TPU v7x, 128 devices: a whole 4x4x4 slice. The times are simulated.
128 devices in a mesh: row: 8 (over y_lo, z), col: 16 (over x, y_hi, core).
Axes of the slice: x: 4, y: 4 (y_hi: 2, y_lo: 2; y = y_hi * 2 + y_lo), z: 4, core: 2. Of those that a mesh axis runs over, the one named last changes fastest.
Arguments:
- inverse: float32 [16384, 16384], P('row', 'col'), may hold values from -0.0625 to 0.0625
- pattern: int32 [128, 128], P('row', 'col'), may hold values 0 or 1
- factor_first: float32 [16384, 256], P('col'), may hold values from -1.5 to 1.5
- factor_second: float32 [16384, 256], P('col'), may hold values from -1.5 to 1.5
- rows_first: int32 [64], replicated, may hold values from 0 to 127, as said below
- rows_second: int32 [64], replicated, may hold values from 0 to 127, as said below
- coupling: float32 [256, 256], replicated, may hold values from -0.375 to 0.375
- diag_first: float32 [256, 256], replicated, may hold values from -6 to 6
- diag_second: float32 [256, 256], replicated, may hold values from -6 to 6
Outputs:
- panel_one: float32 [16384, 256], P(('row', 'col'))
- panel_two: float32 [16384, 256], P(('row', 'col'))
- block_one: float32 [256, 256], replicated
- block_cross: float32 [256, 256], replicated
- block_two: float32 [256, 256], replicated
Inputs may be any that keep to these rules, and one draw needn't show every extreme that they name: `rows_first`: 64 distinct block indices in increasing order; the first block, the block 64 and the last block are always among them. `rows_second`: 64 distinct block indices in increasing order; the first block, the block 64 and the last block are always among them.
All inputs are finite; a program needn't handle non-finite values. No bound on the sum of `pattern` on one device may be relied on, other than what follows from the above.
Results may differ from a plain program's by a relative error of at most 0.000071.
Values sent between devices are 32-bit elements; how exact they have to be, the bound alone decides.
A program may use at most 128 MiB of HBM per device.

v0:
```python
import jax
import jax.numpy as jnp
from jax import lax
from jax.sharding import PartitionSpec as P

BLK = 128


def member(block_ids, rows_list):
    hits = (block_ids[:, None] == rows_list[None, :]).astype(jnp.float32)
    return jnp.sum(hits, axis=1)


def per_device(
    inverse,
    pattern,
    factor_first,
    factor_second,
    rows_first,
    rows_second,
    coupling,
    diag_first,
    diag_second,
):
    high = lax.Precision.HIGHEST
    col_count = lax.axis_size("col")
    row_index = lax.axis_index("row")
    col_index = lax.axis_index("col")
    share_rows = factor_first.shape[0]
    local_rows, local_cols = inverse.shape
    quota_rows = local_rows // col_count
    masked = (
        inverse.reshape(local_rows // BLK, BLK, local_cols // BLK, BLK)
        * pattern.astype(jnp.float32)[:, None, :, None]
    ).reshape(local_rows, local_cols)
    share_ids = (col_index * share_rows + jnp.arange(share_rows, dtype=jnp.int32)) // BLK
    own_start = (row_index * col_count + col_index) * quota_rows
    own_ids = (own_start + jnp.arange(quota_rows, dtype=jnp.int32)) // BLK

    def fetch_rows(factor):
        gathered = lax.all_gather(factor, "col", axis=0, tiled=True)
        return lax.dynamic_slice_in_dim(gathered, own_start, quota_rows, 0)

    def panel_product(factor_kept):
        return lax.psum_scatter(
            jnp.dot(masked, factor_kept, precision=high), "col", scatter_dimension=0, tiled=True
        )

    x_one = factor_first * member(share_ids, rows_first)[:, None]
    x_two = factor_second * member(share_ids, rows_second)[:, None]
    panel_one = -panel_product(x_one)
    near_one = fetch_rows(factor_first)
    near_one = near_one * member(own_ids, rows_first)[:, None]
    first_total = lax.psum(jnp.dot(near_one.T, panel_one, precision=high), ("row", "col"))
    block_one = diag_first - first_total
    near_two = fetch_rows(factor_second)
    near_two = near_two * member(own_ids, rows_second)[:, None]
    panel_two = -(panel_product(x_two) + jnp.dot(panel_one, coupling, precision=high))
    cross_sum, quad_sum = lax.psum(
        (
            jnp.dot(panel_one.T, near_two, precision=high),
            jnp.dot(near_two.T, panel_two, precision=high),
        ),
        ("row", "col"),
    )
    block_cross = -(cross_sum + jnp.dot(block_one, coupling, precision=high))
    block_two = diag_second - quad_sum - jnp.dot(coupling.T, block_cross, precision=high)
    return (panel_one, panel_two, block_one, block_cross, block_two)


def solution(mesh):
    return jax.shard_map(
        per_device,
        mesh=mesh,
        in_specs=(
            P("row", "col"),
            P("row", "col"),
            P("col", None),
            P("col", None),
            P(),
            P(),
            P(),
            P(),
            P(),
        ),
        out_specs=(P(("row", "col"), None), P(("row", "col"), None), P(), P(), P()),
        check_vma=False,
    )
```

profile of v0, /device:TPU:1, one launch (start us, length us, event | category | flops | bytes accessed | tf_op | source)
XLA Modules:
  0.0 555.6 jit_solution(4285565588301605714)
XLA Ops:
  7.2 0.7 convert_element_type.15
  8.0 1.0 convert_reduce_fusion
  9.0 0.6 mul.52
  9.6 3.8 copy-done.1
  13.4 0.1 copy-done.2
  13.5 10.3 %fusion.1 = f32[2048,256]{1,0:T(8,128)} fusion(f32[2048,1024]{1,0:T(8,128)S(1)} %copy-done.2, f32[256,8,8,128]{3,2,1,0:T(8,128)S(1)} %bitcast.19, f32[1024,256]{1,0:T(8,128)} %param.11, f32[1024]{0:T(1024)S(1)} %get-tuple-element.6), kind=kOutput, calls=%fused_computation.2 | convolution fusion | flops 6444810240 | bytes 19927040 | tf_op jit(solution)/shard_map/dot_general | solution.py:46
  23.8 0.2 reduce-scatter.5.cloned.1.call-start
  24.1 12.9 %fusion = f32[2048,256]{1,0:T(8,128)} fusion(f32[2048,1024]{1,0:T(8,128)} %param.9, f32[256,8,8,128]{3,2,1,0:T(8,128)} %bitcast.20, f32[1024,256]{1,0:T(8,128)S(1)} %copy-done.3, f32[1024]{0:T(1024)S(1)} %get-tuple-element.5), kind=kOutput, calls=%fused_computation.1 | convolution fusion | flops 6444810240 | bytes 19927040 | tf_op jit(solution)/shard_map/dot_general | solution.py:46
  37.0 0.7 all-gather.5.cloned.1.call-update
  37.8 0.5 all-gather.3.cloned.1.call-update
  38.4 0.1 convert_reduce_fusion.2
  38.5 57.6 %reduce-scatter.3.cloned.1.call-done = f32[128,256]{1,0:T(8,128)} async-done(((f32[2048,256]{1,0:T(8,128)}), f32[128,256]{1,0:T(8,128)}) %reduce-scatter.3.cloned.1.call-update) | async-done | bytes 131088 | tf_op jit(solution)/shard_map/reduce_scatter | solution.py:45
  96.1 0.9 neg.9
  97.0 73.0 %reduce-scatter.5.cloned.1.call-done = f32[128,256]{1,0:T(8,128)} async-done(((f32[2048,256]{1,0:T(8,128)}), f32[128,256]{1,0:T(8,128)}) %reduce-scatter.5.cloned.1.call-update) | async-done | bytes 131088 | tf_op jit(solution)/shard_map/reduce_scatter | solution.py:45
  170.0 1.2 fusion.4
  171.2 112.4 %all-gather.5.cloned.1.call-done = f32[16384,256]{1,0:T(8,128)} async-done(((f32[1024,256]{1,0:T(8,128)}), f32[16384,256]{1,0:T(8,128)}) %all-gather.5.cloned.1.call-update) | async-done | bytes 16777232 | tf_op jit(solution)/shard_map/all_gather | solution.py:41
  283.5 2.1 fusion.13
  285.6 2.1 fusion.12
  287.7 105.6 %all-gather.3.cloned.1.call-done = f32[16384,256]{1,0:T(8,128)} async-done(((f32[1024,256]{1,0:T(8,128)}), f32[16384,256]{1,0:T(8,128)}) %all-gather.3.cloned.1.call-update) | async-done | bytes 16777232 | tf_op jit(solution)/shard_map/all_gather | solution.py:41
  393.3 2.1 fusion.9
  395.4 148.9 %all-reduce.3.cloned.1.call-done = (f32[256,256]{1,0:T(8,128)}, f32[256,256]{1,0:T(8,128)}, f32[256,256]{1,0:T(8,128)}) async-done(((f32[256,256]{1,0:T(8,128)}, f32[256,256]{1,0:T(8,128)}, f32[256,256]{1,0:T(8,128)}), (f32[256,256]{1,0:T(8,128)}, f32[256,256]{1,0:T(8,128)}, f32[256,256]{1,0:T(8,128)})) %all-reduce.3.cloned.1.call-update) | async-done | bytes 786448 | tf_op jit(solution)/shard_map/psum | solution.py:54
  544.3 1.0 sub.23
  545.3 1.4 fusion.3
  546.7 2.3 fusion.2
  (32 shorter events, 0.4 us)
Async XLA Ops:
  7.2 162.8 %copy-start = (f32[256,256]{1,0:T(8,128)S(1)}, f32[256,256]{1,0:T(8,128)}, u32[]{:S(2)}) copy-start(f32[256,256]{1,0:T(8,128)} %param.15) | copy-start | bytes 786436
  7.2 88.9 %reduce-scatter.3.cloned.1.call-start = ((), (), s32[]{:S(2)}) async-start(), calls=%async_computation.2 | async-start | bytes 2228224 | tf_op jit(solution)/shard_map/reduce_scatter | solution.py:45
  8.0 5.5 copy-start.2
  9.6 3.8 copy-start.1
  13.5 10.5 %copy-start.3 = (f32[1024,256]{1,0:T(8,128)S(1)}, f32[1024,256]{1,0:T(8,128)}, u32[]{:S(2)}) copy-start(f32[1024,256]{1,0:T(8,128)} %param.12) | copy-start | bytes 3145732
  23.8 146.2 %reduce-scatter.5.cloned.1.call-start = ((), (), s32[]{:S(2)}) async-start(), calls=%async_computation.3 | async-start | bytes 2228224 | tf_op jit(solution)/shard_map/reduce_scatter | solution.py:45
  24.0 14.3 %copy-start.10 = (s32[64]{0:T(128)S(1)}, s32[64]{0:T(128)}, u32[]{:S(2)}) copy-start(s32[64]{0:T(128)} %param.14) | copy-start | bytes 772
  24.0 14.3 %copy-start.11 = (s32[64]{0:T(128)S(1)}, s32[64]{0:T(128)}, u32[]{:S(2)}) copy-start(s32[64]{0:T(128)} %param.13) | copy-start | bytes 772
  24.1 520.2 %copy-start.8 = (f32[256,256]{1,0:T(8,128)S(1)}, f32[256,256]{1,0:T(8,128)}, u32[]{:S(2)}) copy-start(f32[256,256]{1,0:T(8,128)} %param.16) | copy-start | bytes 786436
  36.9 509.8 %copy-start.9 = (f32[256,256]{1,0:T(8,128)S(1)}, f32[256,256]{1,0:T(8,128)}, u32[]{:S(2)}) copy-start(f32[256,256]{1,0:T(8,128)} %param.17) | copy-start | bytes 786436
  37.0 246.6 %all-gather.5.cloned.1.call-start = ((), (), s32[]{:S(2)}) async-start(), calls=%async_computation.5 | async-start | bytes 17825792 | tf_op jit(solution)/shard_map/all_gather | solution.py:41
  37.7 355.5 %all-gather.3.cloned.1.call-start = ((), (), s32[]{:S(2)}) async-start(), calls=%async_computation.4 | async-start | bytes 17825792 | tf_op jit(solution)/shard_map/all_gather | solution.py:41
  38.3 506.0 %all-reduce.3.cloned.1.call-start = ((), (), s32[]{:S(2)}) async-start(), calls=%async_computation.6 | async-start | bytes 1572864 | tf_op jit(solution)/shard_map/psum | solution.py:54
  97.0 452.1 %copy-start.4 = (f32[128,256]{1,0:T(8,128)}, f32[128,256]{1,0:T(8,128)S(1)}, u32[]{:S(2)}) copy-start(f32[128,256]{1,0:T(8,128)S(1)} %neg.9) | copy-start | bytes 393220
  171.2 377.9 %copy-start.7 = (f32[128,256]{1,0:T(8,128)}, f32[128,256]{1,0:T(8,128)S(1)}, u32[]{:S(2)}) copy-start(f32[128,256]{1,0:T(8,128)S(1)} %fusion.4) | copy-start | bytes 393220
  545.2 3.8 copy-start.5
  546.7 2.4 copy-start.6
Sparse Core Ops, SparseCore 0:
  23.9 72.0 reduce-scatter.2
  100.0 69.9 reduce-scatter.4
  172.4 111.1 all-gather.4
  285.8 107.4 all-gather.2
  398.7 145.5 all-reduce.2
where the time goes:
time: 556 us
  waiting for transfers between devices  499 us (90%)
  matrix products  34.3 us (6%)
  between operations  14 us (3%)
    all_gather x2, waiting for transfers between devices, fetch_rows(): gathered = lax.all_gather(factor, 'col', axis=0, tiled=True)  218 us
    psum x1, waiting for transfers between devices, per_device(): lax.psum(jnp.dot(near_one.T, panel_one, precision=high), ('row', 'col'))  149 us
    reduce_scatter x2, waiting for transfers between devices, panel_product(): lax.psum_scatter(jnp.dot(masked, factor_kept, precision=high), 'col', sca...  131 us
    dot_general x2, matrix products, panel_product(): jnp.dot(masked, factor_kept, precision=high)  23.1 us
  transfers between devices with their start and end apart: 5, of which 5 were waited for; matrix products, arithmetic and copies ran while one was open for 3% of the time, Pallas kernels for 0%

commit v1 on v0

--- a/solution.py
+++ b/solution.py
@@ -51,7 +51,9 @@
     panel_one = -panel_product(x_one)
     near_one = fetch_rows(factor_first)
     near_one = near_one * member(own_ids, rows_first)[:, None]
-    first_total = lax.psum(jnp.dot(near_one.T, panel_one, precision=high), ("row", "col"))
+    first_total = jnp.sum(
+        lax.all_gather(jnp.dot(near_one.T, panel_one, precision=high), ("row", "col")), axis=0
+    )
     block_one = diag_first - first_total
     near_two = fetch_rows(factor_second)
     near_two = near_two * member(own_ids, rows_second)[:, None]

time: 556 us -> 788 us (1.42)
  waiting for transfers between devices: 499 us -> 719 us
  other arithmetic: 3.66 us -> 14.7 us
    all_gather x0 -> x1, waiting for transfers between devices: none -> 229 us  [per_device(): lax.all_gather(jnp.dot(near_one.T, panel_one, precision=high), ('row', 'c...]
    reduce_sum x0 -> x1, other arithmetic: none -> 12 us  [per_device(): jnp.sum(lax.all_gather(jnp.dot(near_one.T, panel_one, precision=high), ('...]
    psum x1, waiting for transfers between devices: 149 us -> 139 us  [per_device(): lax.psum((jnp.dot(panel_one.T, near_two, precision=high), jnp.dot(near_tw...]
  transfers between devices with their start and end apart: 5 -> 6, of which waited for: 5 -> 6; matrix products, arithmetic and copies ran while one was open for 3% -> 4% of each run, Pallas kernels for 0% -> 0%
where the time goes in v1:
time: 788 us
  waiting for transfers between devices  719 us (91%)
  matrix products  34.2 us (4%)
  other arithmetic  14.7 us (2%)
  between operations  14.3 us (2%)
    all_gather x1, waiting for transfers between devices, per_device(): lax.all_gather(jnp.dot(near_one.T, panel_one, precision=high), ('row', 'c...  229 us
    all_gather x2, waiting for transfers between devices, fetch_rows(): gathered = lax.all_gather(factor, 'col', axis=0, tiled=True)  225 us
    psum x1, waiting for transfers between devices, per_device(): lax.psum((jnp.dot(panel_one.T, near_two, precision=high), jnp.dot(near_tw...  139 us
    reduce_scatter x2, waiting for transfers between devices, panel_product(): lax.psum_scatter(jnp.dot(masked, factor_kept, precision=high), 'col', sca...  126 us
    dot_general x2, matrix products, panel_product(): jnp.dot(masked, factor_kept, precision=high)  23.1 us
  transfers between devices with their start and end apart: 6, of which 6 were waited for; matrix products, arithmetic and copies ran while one was open for 4% of the time, Pallas kernels for 0%

profile of v1, /device:TPU:1, one launch (start us, length us, event | category | flops | bytes accessed | tf_op | source)
XLA Modules:
  0.0 787.7 jit_solution(17072713600558346799)
XLA Ops:
  7.2 0.7 convert_element_type.15
  8.0 1.0 convert_reduce_fusion
  9.0 0.6 mul.52
  9.6 3.8 copy-done.1
  13.5 10.3 %fusion.1 = f32[2048,256]{1,0:T(8,128)} fusion(f32[2048,1024]{1,0:T(8,128)S(1)} %copy-done.2, f32[256,8,8,128]{3,2,1,0:T(8,128)S(1)} %bitcast.20, f32[1024,256]{1,0:T(8,128)} %param.11, f32[1024]{0:T(1024)S(1)} %get-tuple-element.6), kind=kOutput, calls=%fused_computation.2 | convolution fusion | flops 6444810240 | bytes 19927040 | tf_op jit(solution)/shard_map/dot_general | solution.py:46
  23.8 0.7 all-gather.5.cloned.1.call-update
  24.6 0.2 reduce-scatter.5.cloned.1.call-start
  24.8 12.8 %fusion = f32[2048,256]{1,0:T(8,128)} fusion(f32[2048,1024]{1,0:T(8,128)} %param.9, f32[256,8,8,128]{3,2,1,0:T(8,128)} %bitcast.21, f32[1024,256]{1,0:T(8,128)S(1)} %copy-done.3, f32[1024]{0:T(1024)S(1)} %get-tuple-element.5), kind=kOutput, calls=%fused_computation.1 | convolution fusion | flops 6444810240 | bytes 19927040 | tf_op jit(solution)/shard_map/dot_general | solution.py:46
  37.7 0.5 all-gather.7.cloned.1.call-update
  38.3 0.1 convert_reduce_fusion.2
  38.4 57.6 %reduce-scatter.3.cloned.1.call-done = f32[128,256]{1,0:T(8,128)} async-done(((f32[2048,256]{1,0:T(8,128)}), f32[128,256]{1,0:T(8,128)}) %reduce-scatter.3.cloned.1.call-update) | async-done | bytes 131088 | tf_op jit(solution)/shard_map/reduce_scatter | solution.py:45
  96.0 0.9 neg.9
  97.0 112.6 %all-gather.5.cloned.1.call-done = f32[16384,256]{1,0:T(8,128)} async-done(((f32[1024,256]{1,0:T(8,128)}), f32[16384,256]{1,0:T(8,128)}) %all-gather.5.cloned.1.call-update) | async-done | bytes 16777232 | tf_op jit(solution)/shard_map/all_gather | solution.py:41
  209.6 2.1 fusion.9
  211.8 68.0 %reduce-scatter.5.cloned.1.call-done = f32[128,256]{1,0:T(8,128)} async-done(((f32[2048,256]{1,0:T(8,128)}), f32[128,256]{1,0:T(8,128)}) %reduce-scatter.5.cloned.1.call-update) | async-done | bytes 131088 | tf_op jit(solution)/shard_map/reduce_scatter | solution.py:45
  279.8 1.2 fusion.4
  281.0 112.2 %all-gather.7.cloned.1.call-done = f32[16384,256]{1,0:T(8,128)} async-done(((f32[1024,256]{1,0:T(8,128)}), f32[16384,256]{1,0:T(8,128)}) %all-gather.7.cloned.1.call-update) | async-done | bytes 16777232 | tf_op jit(solution)/shard_map/all_gather | solution.py:41
  393.2 2.1 fusion.13
  395.3 2.1 fusion.12
  397.4 228.6 %all-gather.9.cloned.1.call-done = f32[32768,256]{1,0:T(8,128)} async-done(((f32[256,256]{1,0:T(8,128)}), f32[32768,256]{1,0:T(8,128)}) %all-gather.9.cloned.1.call-update) | async-done | bytes 33554448 | tf_op jit(solution)/shard_map/all_gather | solution.py:55
  626.0 12.0 %reduce_sum.48 = f32[256,256]{1,0:T(8,128)S(1)} reduce(f32[128,256,256]{2,1,0:T(8,128)} %bitcast.22, f32[]{:T(128)} %constant.38.clone.1), dimensions={0}, to_apply=%region_5.6 | reduce | flops 8323072 | bytes 33816580 | tf_op jit(solution)/shard_map/reduce_sum | solution.py:54
  638.1 139.1 %all-reduce.3.cloned.1.call-done = (f32[256,256]{1,0:T(8,128)}, f32[256,256]{1,0:T(8,128)}) async-done(((f32[256,256]{1,0:T(8,128)}, f32[256,256]{1,0:T(8,128)}), (f32[256,256]{1,0:T(8,128)}, f32[256,256]{1,0:T(8,128)})) %all-reduce.3.cloned.1.call-update) | async-done | bytes 524304 | tf_op jit(solution)/shard_map/psum | solution.py:61
  777.2 1.3 fusion.3
  778.5 2.3 fusion.2
  (36 shorter events, 0.5 us)
Async XLA Ops:
  7.2 272.6 %copy-start = (f32[256,256]{1,0:T(8,128)S(1)}, f32[256,256]{1,0:T(8,128)}, u32[]{:S(2)}) copy-start(f32[256,256]{1,0:T(8,128)} %param.15) | copy-start | bytes 786436
  7.2 88.9 %reduce-scatter.3.cloned.1.call-start = ((), (), s32[]{:S(2)}) async-start(), calls=%async_computation.2 | async-start | bytes 2228224 | tf_op jit(solution)/shard_map/reduce_scatter | solution.py:45
  8.0 5.5 copy-start.2
  9.6 3.8 copy-start.1
  13.5 11.3 %copy-start.3 = (f32[1024,256]{1,0:T(8,128)S(1)}, f32[1024,256]{1,0:T(8,128)}, u32[]{:S(2)}) copy-start(f32[1024,256]{1,0:T(8,128)} %param.12) | copy-start | bytes 3145732
  23.8 185.8 %all-gather.5.cloned.1.call-start = ((), (), s32[]{:S(2)}) async-start(), calls=%async_computation.4 | async-start | bytes 17825792 | tf_op jit(solution)/shard_map/all_gather | solution.py:41
  24.6 255.2 %reduce-scatter.5.cloned.1.call-start = ((), (), s32[]{:S(2)}) async-start(), calls=%async_computation.3 | async-start | bytes 2228224 | tf_op jit(solution)/shard_map/reduce_scatter | solution.py:45
  24.8 13.5 %copy-start.10 = (s32[64]{0:T(128)S(1)}, s32[64]{0:T(128)}, u32[]{:S(2)}) copy-start(s32[64]{0:T(128)} %param.14) | copy-start | bytes 772
  24.8 13.5 %copy-start.11 = (s32[64]{0:T(128)S(1)}, s32[64]{0:T(128)}, u32[]{:S(2)}) copy-start(s32[64]{0:T(128)} %param.13) | copy-start | bytes 772
  37.7 355.6 %all-gather.7.cloned.1.call-start = ((), (), s32[]{:S(2)}) async-start(), calls=%async_computation.5 | async-start | bytes 17825792 | tf_op jit(solution)/shard_map/all_gather | solution.py:41
  38.2 587.8 %all-gather.9.cloned.1.call-start = ((), (), s32[]{:S(2)}) async-start(), calls=%async_computation.6 | async-start | bytes 33816576 | tf_op jit(solution)/shard_map/all_gather | solution.py:55
  96.9 541.1 %copy-start.4 = (f32[128,256]{1,0:T(8,128)}, f32[128,256]{1,0:T(8,128)S(1)}, u32[]{:S(2)}) copy-start(f32[128,256]{1,0:T(8,128)S(1)} %neg.9) | copy-start | bytes 393220
  211.7 565.5 %all-reduce.3.cloned.1.call-start = ((), (), s32[]{:S(2)}) async-start(), calls=%async_computation.7 | async-start | bytes 1048576 | tf_op jit(solution)/shard_map/psum | solution.py:61
  281.0 357.0 %copy-start.7 = (f32[128,256]{1,0:T(8,128)}, f32[128,256]{1,0:T(8,128)S(1)}, u32[]{:S(2)}) copy-start(f32[128,256]{1,0:T(8,128)S(1)} %fusion.4) | copy-start | bytes 393220
  626.0 12.0 %copy-start.8 = (f32[256,256]{1,0:T(8,128)S(1)}, f32[256,256]{1,0:T(8,128)}, u32[]{:S(2)}) copy-start(f32[256,256]{1,0:T(8,128)} %param.16) | copy-start | bytes 786436
  626.0 152.5 %copy-start.9 = (f32[256,256]{1,0:T(8,128)S(1)}, f32[256,256]{1,0:T(8,128)}, u32[]{:S(2)}) copy-start(f32[256,256]{1,0:T(8,128)} %param.17) | copy-start | bytes 786436
  638.1 142.8 %copy-start.5 = (f32[256,256]{1,0:T(8,128)}, f32[256,256]{1,0:T(8,128)S(1)}, u32[]{:S(2)}) copy-start(f32[256,256]{1,0:T(8,128)S(1)} %sub.23) | copy-start | bytes 786436
  778.5 2.4 copy-start.6
Sparse Core Ops, SparseCore 0:
  23.9 72.0 reduce-scatter.2
  98.4 111.1 all-gather.4
  213.5 66.1 reduce-scatter.4
  282.0 111.1 all-gather.6
  395.4 230.6 all-gather.8
  631.4 145.7 all-reduce.2
